TPU v7x, 256 devices: a whole 4x4x8 slice. The times are simulated.
256 devices in a mesh: vol: 64 (over z, y, core), dsg: 4 (over x).
Axes of the slice: x: 4, y: 4, z: 8, core: 2. Of those that a mesh axis runs over, the one named last changes fastest.
Arguments:
- fields: float32 [262144, 128], P('vol'), may hold values from -6 to 6
- far_geom: float32 [8, 131072], P(None, ('vol', 'dsg')), may hold values from -6 to 6, as said below
- far_block: int32 [131072, 1], P(('vol', 'dsg')), may hold values from 0 to 63; in each aligned block of 512 rows (0 to 511, 512 to 1023, ...) at most 20 rows name the same one
- far_cell: int32 [131072], P(('vol', 'dsg')), may hold values from 0 to 4095
- far_patch: int32 [131072], P(('vol', 'dsg')), may hold values from 0 to 95, as said below
- near_geom: float32 [8, 524288], P(None, ('vol', 'dsg')), may hold values from -6 to 6, as said below
- near_cell: int32 [524288], P(('vol', 'dsg')), may hold values from 0 to 4095
- near_patch: int32 [524288], P(('vol', 'dsg')), may hold values from 0 to 95, as said below
- adjacency: int32 [96, 4], replicated, may hold values from -1 to 95, as said below
Outputs:
- far_density: float32 [131072], P(('vol', 'dsg'))
- design_grad: float32 [96, 64, 64], P('dsg')
Inputs may be any that keep to these rules, and one draw needn't show every extreme that they name: `far_geom`: rows 0-2 and 6-7 lie in [0, 1). `near_geom`: rows 0-2 and 6-7 lie in [0, 1). `far_block`: the 512 far points of one device name each block at most 20 times. `far_patch`: the far and near points of one device lie on at most 4 design patches, the same set for both. `near_patch`: the far and near points of one device lie on at most 4 design patches, the same set for both. -1 marks a free side; where adjacency[k, s] = m >= 0, adjacency[m, s xor 1] = k.
All inputs are finite; a program needn't handle non-finite values.
Results may differ from a plain program's by a relative error of at most 0.0003.
Values sent between devices are 32-bit elements; how exact they have to be, the bound alone decides.
A program may use at most 128 MiB of HBM per device.

v0:
```python
import jax
import jax.numpy as jnp
import numpy as np
from jax import lax
from jax.sharding import PartitionSpec as P

CTRL = 64
PATCH_GRP = 4
SMOOTH_ITERS = 3
PENALTY = 4.0
SMOOTHING = 16.0
FLIPPED = np.array([1, 0, 3, 2], dtype=np.int32)


def bernstein(position):
    complement = 1.0 - position
    values = jnp.stack(
        [
            complement * complement * complement,
            3.0 * position * complement * complement,
            3.0 * position * position * complement,
            position * position * position,
        ]
    )
    slopes = jnp.stack(
        [
            -3.0 * complement * complement,
            3.0 * complement * complement - 6.0 * position * complement,
            6.0 * position * complement - 3.0 * position * position,
            3.0 * position * position,
        ]
    )
    return (values, slopes)


def tensor_basis(factor_x, factor_y, factor_z):
    product = factor_x[:, None, None, :] * factor_y[None, :, None, :] * factor_z[None, None, :, :]
    return product.reshape(-1, factor_x.shape[-1])


def evaluate(columns, coords):
    value_x, slope_x = bernstein(coords[0])
    value_y, slope_y = bernstein(coords[1])
    value_z, slope_z = bernstein(coords[2])
    basis_set = [
        tensor_basis(value_x, value_y, value_z),
        tensor_basis(slope_x, value_y, value_z),
        tensor_basis(value_x, slope_y, value_z),
        tensor_basis(value_x, value_y, slope_z),
    ]
    half_width = columns.shape[0] // 2
    state_part = columns[:half_width]
    adjoint_part = columns[half_width:]
    results = [jnp.sum(state_part * basis_kind, 0) for basis_kind in basis_set]
    results = results + [jnp.sum(adjoint_part * basis_kind, 0) for basis_kind in basis_set]
    return jnp.stack(results)


def density(values, normals):
    grad_state = values[1:4]
    grad_adjoint = values[5:8]
    normal_sq = jnp.sum(normals * normals, 0)
    inner_sum = jnp.sum(grad_state * grad_adjoint, 0)
    along_state = jnp.sum(grad_state * normals, 0)
    along_adjoint = jnp.sum(grad_adjoint * normals, 0)
    return (
        normal_sq * inner_sum
        - 2.0 * along_state * along_adjoint
        + PENALTY * normal_sq * values[0] * values[4]
    )


def spline_weights(param, span_count):
    scaled = param * span_count
    first_span = jnp.clip(jnp.floor(scaled), 0, span_count - 1)
    offset_in = scaled - first_span
    complement = 1.0 - offset_in
    cubed = offset_in * offset_in * offset_in
    squared = offset_in * offset_in
    weights = jnp.stack(
        [
            complement * complement * complement / 6.0,
            (3.0 * cubed - 6.0 * squared + 4.0) / 6.0,
            (-3.0 * cubed + 3.0 * squared + 3.0 * offset_in + 1.0) / 6.0,
            cubed / 6.0,
        ]
    )
    return (first_span.astype(jnp.int32), weights)


def spline_matrix(param, control):
    start, weights = spline_weights(param, control - 3)
    columns = jnp.arange(control, dtype=jnp.int32)
    matrix = jnp.zeros((param.shape[0], control), jnp.float32)
    for offset in range(4):
        matrix = matrix + jnp.where(
            (start + offset)[:, None] == columns[None, :], weights[offset][:, None], 0.0
        )
    return matrix


def local_grid(strength, spline_params, patch_ids, slot_ids, slot_live, control):
    weights_s = spline_matrix(spline_params[0], control)
    weights_t = spline_matrix(spline_params[1], control)
    selector = ((patch_ids[:, None] == slot_ids[None, :]) & slot_live[None, :]).astype(jnp.float32)
    left = ((selector * strength[:, None])[:, :, None] * weights_s[:, None, :]).reshape(
        strength.shape[0], -1
    )
    result = jnp.einsum(
        "na,nb->ab",
        left,
        weights_t,
        precision=lax.Precision.HIGHEST,
        preferred_element_type=jnp.float32,
    )
    return result.reshape(slot_ids.shape[0], control, control)


def edge_table(iterate):
    return jnp.stack([iterate[:, 0, :], iterate[:, -1, :], iterate[:, :, 0], iterate[:, :, -1]], 1)


def lookup(edge_rows, neighbours):
    total_rows = edge_rows.shape[0] * 4
    wanted = (neighbours * 4 + FLIPPED[None, :]).reshape(-1)
    present = (neighbours >= 0).reshape(-1)
    selector = (
        (wanted[:, None] == jnp.arange(total_rows, dtype=jnp.int32)[None, :]) & present[:, None]
    ).astype(jnp.float32)
    picked = jnp.dot(
        selector,
        edge_rows.reshape(total_rows, -1),
        precision=lax.Precision.HIGHEST,
        preferred_element_type=jnp.float32,
    )
    return picked.reshape(neighbours.shape[0], 4, -1)


def apply_operator(iterate, halo_rows):
    patch_count, edge_size = (iterate.shape[0], iterate.shape[1])
    padded = jnp.zeros((patch_count, edge_size + 2, edge_size + 2), iterate.dtype)
    padded = padded.at[:, 1:-1, 1:-1].set(iterate)
    padded = padded.at[:, 0, 1:-1].set(halo_rows[:, 0])
    padded = padded.at[:, -1, 1:-1].set(halo_rows[:, 1])
    padded = padded.at[:, 1:-1, 0].set(halo_rows[:, 2])
    padded = padded.at[:, 1:-1, -1].set(halo_rows[:, 3])
    beside = padded[:, :-2, 1:-1] + padded[:, 2:, 1:-1] + padded[:, 1:-1, :-2] + padded[:, 1:-1, 2:]
    return iterate + SMOOTHING * (4.0 * iterate - beside)


def precondition(residual):
    patch_count, edge_size = (residual.shape[0], residual.shape[1])
    below_diag = jnp.full((patch_count, edge_size), -SMOOTHING, residual.dtype).at[:, 0].set(0.0)
    main_diag = jnp.full((patch_count, edge_size), 1.0 + 2.0 * SMOOTHING, residual.dtype)
    above_diag = jnp.full((patch_count, edge_size), -SMOOTHING, residual.dtype).at[:, -1].set(0.0)
    along_rows = lax.linalg.tridiagonal_solve(below_diag, main_diag, above_diag, residual)
    along_cols = lax.linalg.tridiagonal_solve(
        below_diag, main_diag, above_diag, jnp.swapaxes(along_rows, 1, 2)
    )
    return jnp.swapaxes(along_cols, 1, 2)


def keep_table(edge_rows):
    return edge_rows


def smooth(summed, neighbours, edges_of):
    iterate = precondition(summed)
    for sweep_index in range(SMOOTH_ITERS):
        halo_rows = lookup(edges_of(edge_table(iterate)), neighbours)
        iterate = iterate + precondition(summed - apply_operator(iterate, halo_rows))
    return iterate


def per_device(
    fields, far_geom, far_block, far_cell, far_patch, near_geom, near_cell, near_patch, adjacency
):
    vol_count = lax.axis_size("vol")
    far_count = far_cell.shape[0]
    capacity = 5 * far_count // (2 * vol_count)
    patches = adjacency.shape[0]
    control = CTRL
    group = PATCH_GRP
    patch_range = jnp.arange(patches, dtype=jnp.int32)
    present = jnp.any(near_patch[:, None] == patch_range[None, :], 0)
    present = present | jnp.any(far_patch[:, None] == patch_range[None, :], 0)
    rank = jnp.cumsum(present.astype(jnp.int32)) - 1
    matches = present[None, :] & (rank[None, :] == jnp.arange(group, dtype=jnp.int32)[:, None])
    slot_ids = jnp.sum(matches.astype(jnp.int32) * patch_range[None, :], 1)
    slot_live = jnp.any(matches, 1)
    near_count = near_cell.shape[0]
    block_len = min(4096, near_count)
    blocks = near_count // block_len

    def near_block(carried, inputs):
        geom_part, cells_part, patch_part = inputs
        rows = jnp.take(fields, cells_part, axis=0).T
        strength = density(evaluate(rows, geom_part[0:3]), geom_part[3:6])
        return (
            carried
            + local_grid(strength, geom_part[6:8], patch_part, slot_ids, slot_live, control),
            None,
        )

    start_grid = jnp.zeros((group, control, control), jnp.float32)
    grid_local, unused = lax.scan(
        near_block,
        start_grid,
        (
            near_geom.reshape(8, blocks, block_len).transpose(1, 0, 2),
            near_cell.reshape(blocks, block_len),
            near_patch.reshape(blocks, block_len),
        ),
    )
    target = far_block[:, 0]
    onehot_dest = (target[:, None] == jnp.arange(vol_count, dtype=jnp.int32)[None, :]).astype(
        jnp.int32
    )
    before = jnp.cumsum(onehot_dest, 0) - onehot_dest
    slot_rank = jnp.sum(before * onehot_dest, 1)
    slot_of = target * capacity + slot_rank
    request = jnp.zeros((1, vol_count * capacity), jnp.int32).at[0, slot_of].set(far_cell)
    request = request.reshape(1, vol_count, capacity)
    incoming = lax.all_to_all(request, "vol", split_axis=1, concat_axis=1, tiled=True)
    picked = jnp.take(fields, incoming.reshape(-1), axis=0).T
    picked = picked.reshape(fields.shape[1], incoming.shape[1], incoming.shape[2])
    replies = lax.all_to_all(picked, "vol", split_axis=1, concat_axis=1, tiled=True)
    placed = jnp.zeros((3, vol_count * capacity), jnp.float32).at[:, slot_of].set(far_geom[0:3])
    slot_values = evaluate(replies.reshape(replies.shape[0], -1), placed)
    far_values = jnp.take(slot_values, slot_of, axis=1)
    far_strength = density(far_values, far_geom[3:6])
    grid_local = grid_local + local_grid(
        far_strength, far_geom[6:8], far_patch, slot_ids, slot_live, control
    )
    placing = ((patch_range[:, None] == slot_ids[None, :]) & slot_live[None, :]).astype(jnp.float32)
    owner_count = lax.axis_size("dsg")
    per_owner = patches // owner_count
    owner_index = lax.axis_index("dsg")
    grid_whole = jnp.dot(
        placing,
        grid_local.reshape(group, -1),
        precision=lax.Precision.HIGHEST,
        preferred_element_type=jnp.float32,
    )
    summed = lax.psum(grid_whole, ("vol", "dsg")).reshape(patches, control, control)
    design = smooth(summed, adjacency, keep_table)
    design = lax.dynamic_slice_in_dim(design, owner_index * per_owner, per_owner, 0)
    return (far_strength, design)


def solution(mesh):
    return jax.shard_map(
        per_device,
        mesh=mesh,
        in_specs=(
            P("vol", None),
            P(None, ("vol", "dsg")),
            P(("vol", "dsg"), None),
            P(("vol", "dsg")),
            P(("vol", "dsg")),
            P(None, ("vol", "dsg")),
            P(("vol", "dsg")),
            P(("vol", "dsg")),
            P(),
        ),
        out_specs=(P(("vol", "dsg")), P("dsg", None, None)),
        check_vma=False,
    )
```

profile of v0, /device:TPU:2, one launch (start us, length us, event | category | flops | bytes accessed | tf_op | source)
XLA Modules:
  0.0 598.5 jit_solution(6945396377052510805)
XLA Ops:
  11.5 2.6 scatter_custom_fusion
  14.9 12.1 %all-to-all-start = ((s32[1,64,20]{2,0,1:T(1,128)}), s32[1,64,20]{2,0,1:T(1,128)S(1)}, u32[]{:S(2)}, u32[]{:S(2)}) async-start(s32[1,64,20]{2,0,1:T(1,128)} %bitcast.5), calls=%async_computation | async-start | bytes 65536 | tf_op jit(solution)/shard_map/all_to_all | solution.py:224
  68.9 4.6 mul.70848
  73.6 3.5 copy.7280
  77.1 4.4 mul.70860
  81.5 3.6 copy.7281
  85.1 4.4 mul.70872
  89.6 3.6 copy.7282
  93.1 3.8 mul.70882
  96.9 3.5 copy.7283
  100.7 7.6 %gather_fusion.2 = f32[2048,128]{1,0:T(8,128)} fusion(f32[4096,128]{1,0:T(8,128)S(1)} %copy-done, s32[2048]{0:T(1024)S(1)} %get-tuple-element.1882), kind=kCustom, calls=%fused_computation.2 | custom fusion | bytes 2105344 | tf_op jit(solution)/shard_map/while/body/eval_jaxpr/jit(_take)/gather | solution.py:197
  108.4 3.1 gather_fusion
  115.1 10.4 %all-to-all-start.1 = ((f32[128,64,20]{0,2,1:T(8,128)}), f32[128,64,20]{0,2,1:T(8,128)S(1)}, u32[]{:S(2)}, u32[]{:S(2)}) async-start(f32[128,64,20]{0,2,1:T(8,128)} %reshape.315135), calls=%async_computation.1 | async-start | bytes 1572864 | tf_op jit(solution)/shard_map/all_to_all | solution.py:227
  127.9 2.6 multiply_reduce_fusion.7
  130.8 18.1 %all-to-all-done.1 = f32[128,64,20]{0,2,1:T(8,128)S(1)} async-done(((f32[128,64,20]{0,2,1:T(8,128)}), f32[128,64,20]{0,2,1:T(8,128)S(1)}, u32[]{:S(2)}, u32[]{:S(2)}) %all-to-all-start.1) | async-done | bytes 655392 | tf_op jit(solution)/shard_map/all_to_all | solution.py:227
  148.8 3.8 multiply_reduce_fusion.8
  159.1 3.1 fusion.83
  163.0 257.5 %all-reduce.6.cloned.1.call-done = f32[96,64,64]{0,2,1:T(8,128)} async-done(((f32[96,64,64]{0,2,1:T(8,128)}), f32[96,64,64]{0,2,1:T(8,128)}) %all-reduce.6.cloned.1.call-update) | async-done | bytes 1572880 | tf_op jit(solution)/shard_map/psum | solution.py:245
  437.5 4.8 multiply_subtract_fusion.370
  442.4 9.9 %concatenate.199 = f32[63,96,64]{1,0,2:T(8,128)S(1)} concatenate(f32[1,96,64]{1,0,2:T(1,128)} %get-tuple-element.1225, f32[1,96,64]{1,0,2:T(1,128)} %get-tuple-element.1226, f32[1,96,64]{1,0,2:T(1,128)} %get-tuple-element.1227, f32[1,96,64]{1,0,2:T(1,128)} %get-tuple-element.1228, f32[1,96,64]{1,0,2:T(1,128)} %get-tuple-element.1229, f32[1,96,64]{1,0,2:T(1,128)} %get-tuple-element.1230, ...), dimensions={0} | concatenate | bytes 3096576 | tf_op jit(solution)/shard_map/vmap()/concatenate | solution.py:156
  463.7 3.3 fusion.11
  469.4 2.7 multiply_subtract_fusion.308
  476.5 2.7 broadcast_multiply_fusion.14
  494.9 3.0 fusion.7
  515.1 4.7 multiply_subtract_fusion.124
  519.8 15.6 %concatenate.207 = f32[63,96,64]{1,0,2:T(8,128)} concatenate(f32[1,96,64]{1,0,2:T(1,128)S(1)} %get-tuple-element.820, f32[1,96,64]{1,0,2:T(1,128)S(1)} %get-tuple-element.821, f32[1,96,64]{1,0,2:T(1,128)S(1)} %get-tuple-element.822, f32[1,96,64]{1,0,2:T(1,128)} %get-tuple-element.823, f32[1,96,64]{1,0,2:T(1,128)} %get-tuple-element.824, f32[1,96,64]{1,0,2:T(1,128)} %get-tuple-element.825, ...), dimensions={0} | concatenate | bytes 3096576 | tf_op jit(solution)/shard_map/vmap()/concatenate | solution.py:156
  546.4 3.0 fusion.3
  552.6 4.3 multiply_subtract_fusion.62
  569.4 4.9 multiply_subtract_fusion
  574.4 9.8 %concatenate.211 = f32[63,96,64]{1,0,2:T(8,128)S(1)} concatenate(f32[1,96,64]{1,0,2:T(1,128)S(1)} %get-tuple-element.656, f32[1,96,64]{1,0,2:T(1,128)S(1)} %get-tuple-element.657, f32[1,96,64]{1,0,2:T(1,128)S(1)} %get-tuple-element.658, f32[1,96,64]{1,0,2:T(1,128)} %get-tuple-element.659, f32[1,96,64]{1,0,2:T(1,128)} %get-tuple-element.660, f32[1,96,64]{1,0,2:T(1,128)} %get-tuple-element.661, ...), dimensions={0} | concatenate | bytes 3096576 | tf_op jit(solution)/shard_map/vmap()/concatenate | solution.py:156
  585.8 2.5 dynamic-slice_add_fusion
  588.2 3.2 copy.8826
  (894 shorter events, 151.3 us)
Async XLA Ops:
  7.2 93.6 %copy-start = (f32[4096,128]{1,0:T(8,128)S(1)}, f32[4096,128]{1,0:T(8,128)}, u32[]{:S(2)}) copy-start(f32[4096,128]{1,0:T(8,128)} %param.58) | copy-start | bytes 6291460
  11.5 30.1 %copy-start.118 = (s32[512,1]{0,1:T(1,128)}, s32[512,1]{0,1:T(1,128)S(1)}, u32[]{:S(2)}) copy-start(s32[512,1]{0,1:T(1,128)S(1)} %get-tuple-element.1367) | copy-start | bytes 6148
  14.9 85.7 %all-to-all-start = ((s32[1,64,20]{2,0,1:T(1,128)}), s32[1,64,20]{2,0,1:T(1,128)S(1)}, u32[]{:S(2)}, u32[]{:S(2)}) async-start(s32[1,64,20]{2,0,1:T(1,128)} %bitcast.5), calls=%async_computation | async-start | bytes 65536 | tf_op jit(solution)/shard_map/all_to_all | solution.py:224
  48.9 4.5 copy-start.119
  93.1 7.3 %copy-start.102 = (f32[3,512]{1,0:T(4,128)S(1)}, f32[3,512]{1,0:T(4,128)}, u32[]{:S(2)}) copy-start(f32[3,512]{1,0:T(4,128)} %get-tuple-element.1815) | copy-start | bytes 18436
  112.9 13.2 %copy-start.109 = (pred[2048]{0:T(1024)(128)(4,1)S(1)}, pred[2048]{0:T(1024)(128)(4,1)}, u32[]{:S(2)}) copy-start(pred[2048]{0:T(1024)(128)(4,1)} %compare_and_fusion) | copy-start | bytes 6148
  115.1 12.6 %copy-start.8 = (f32[64,2048]{0,1:T(8,128)S(1)}, f32[64,2048]{0,1:T(8,128)}, u32[]{:S(2)}) copy-start(f32[64,2048]{0,1:T(8,128)} %copy.7291) | copy-start | bytes 1572868
  115.1 33.7 %all-to-all-start.1 = ((f32[128,64,20]{0,2,1:T(8,128)}), f32[128,64,20]{0,2,1:T(8,128)S(1)}, u32[]{:S(2)}, u32[]{:S(2)}) async-start(f32[128,64,20]{0,2,1:T(8,128)} %reshape.315135), calls=%async_computation.1 | async-start | bytes 1572864 | tf_op jit(solution)/shard_map/all_to_all | solution.py:227
  125.6 294.9 %all-reduce.6.cloned.1.call-start = ((), (), s32[]{:S(2)}) async-start(), calls=%async_computation.2 | async-start | bytes 4194304 | tf_op jit(solution)/shard_map/psum | solution.py:245
  130.8 24.3 %copy-start.133 = (pred[512]{0:T(512)(128)(4,1)S(1)}, pred[512]{0:T(512)(128)(4,1)}, u32[]{:S(2)}) copy-start(pred[512]{0:T(512)(128)(4,1)} %get-tuple-element.1366) | copy-start | bytes 1540
  152.7 4.1 copy-start.79
  152.7 4.1 copy-start.123
  152.7 4.1 copy-start.124
  152.8 4.1 copy-start.125
  152.8 4.1 copy-start.126
  152.8 4.1 copy-start.127
  152.8 4.1 copy-start.128
  152.8 4.1 copy-start.129
  156.1 6.2 %copy-start.122 = (f32[512]{0:T(512)}, f32[512]{0:T(512)S(1)}, u32[]{:S(2)}) copy-start(f32[512]{0:T(512)S(1)} %multiply_add_fusion.2) | copy-start | bytes 6148
  431.2 11.1 %copy-start.80 = (f32[96,64]{0,1:T(8,128)}, f32[96,64]{0,1:T(8,128)S(1)}, u32[]{:S(2)}) copy-start(f32[96,64]{0,1:T(8,128)S(1)} %get-tuple-element.1210) | copy-start | bytes 73732
  431.2 11.1 %copy-start.83 = (f32[96,64]{0,1:T(8,128)}, f32[96,64]{0,1:T(8,128)S(1)}, u32[]{:S(2)}) copy-start(f32[96,64]{0,1:T(8,128)S(1)} %get-tuple-element.1211) | copy-start | bytes 73732
  431.2 21.0 %copy-start.75 = (f32[96,64]{0,1:T(8,128)}, f32[96,64]{0,1:T(8,128)S(1)}, u32[]{:S(2)}) copy-start(f32[96,64]{0,1:T(8,128)S(1)} %get-tuple-element.1202) | copy-start | bytes 73732
  437.3 5.0 copy-start.11
  437.4 4.9 copy-start.15
  437.4 4.9 copy-start.19
  437.4 4.9 copy-start.23
  437.4 4.9 copy-start.27
  437.5 4.9 copy-start.31
  519.8 15.6 %copy-start.5 = (f32[96,64,64]{0,2,1:T(8,128)S(1)}, f32[96,64,64]{0,2,1:T(8,128)}, u32[]{:S(2)}) copy-start(f32[96,64,64]{0,2,1:T(8,128)} %copy-done.4) | copy-start | bytes 4718596
  519.8 15.6 %copy-start.86 = (f32[96,64]{0,1:T(8,128)S(1)}, f32[96,64]{0,1:T(8,128)}, u32[]{:S(2)}) copy-start(f32[96,64]{0,1:T(8,128)} %get-tuple-element.800) | copy-start | bytes 73732
  574.4 9.8 %copy-start.85 = (f32[96,64]{0,1:T(8,128)S(1)}, f32[96,64]{0,1:T(8,128)}, u32[]{:S(2)}) copy-start(f32[96,64]{0,1:T(8,128)} %get-tuple-element.636) | copy-start | bytes 73732
  585.8 5.6 copy-start.1
  (114 other events, 235.0 us)
Sparse Core Ops, SparseCore 0:
  162.4 258.0 all-reduce.5
where the time goes:
time: 609 us; the launch traced here: 599 us
  waiting for transfers between devices  276 us (45%)
  local copies, waits for them, and re-layouts  155 us (25%)
  other arithmetic  114 us (19%)
  starting transfers between devices  23 us (4%)
  between operations  20.4 us (3%)
  matrix products  10.6 us (2%)
    psum x1, waiting for transfers between devices, per_device(): lax.psum(grid_whole, ('vol', 'dsg')).reshape(patches, control, control)  258 us
    mul x16, local copies, waits for them, and re-layouts, tensor_basis(): factor_x[:, None, None, :] * factor_y[None, :, None, :]  47 us
    sub x37, other arithmetic, precondition(): lax.linalg.tridiagonal_solve(below_diag, main_diag, above_diag, residual)  42 us
    concatenate x3, local copies, waits for them, and re-layouts, precondition(): lax.linalg.tridiagonal_solve(below_diag, main_diag, above_diag, residual)  35.3 us
    all_to_all x1, waiting for transfers between devices, per_device(): lax.all_to_all(picked, 'vol', split_axis=1, concat_axis=1, tiled=True)  18.1 us
    unnamed x515, local copies, waits for them, and re-layouts  16 us
  transfers between devices with their start and end apart: 3, of which 2 were waited for; matrix products, arithmetic and copies ran while one was open for 13% of the time, Pallas kernels for 0%

commit v1 on v0

--- a/solution.py
+++ b/solution.py
@@ -221,7 +221,10 @@
     slot_of = target * capacity + slot_rank
     request = jnp.zeros((1, vol_count * capacity), jnp.int32).at[0, slot_of].set(far_cell)
     request = request.reshape(1, vol_count, capacity)
-    incoming = lax.all_to_all(request, "vol", split_axis=1, concat_axis=1, tiled=True)
+    incoming = jnp.concatenate(
+        lax.all_to_all(jnp.stack(jnp.split(request, lax.axis_size("vol"), axis=1)), "vol", 0, 0),
+        axis=1,
+    )
     picked = jnp.take(fields, incoming.reshape(-1), axis=0).T
     picked = picked.reshape(fields.shape[1], incoming.shape[1], incoming.shape[2])
     replies = lax.all_to_all(picked, "vol", split_axis=1, concat_axis=1, tiled=True)

time: 609 us -> 644 us (1.057)
  local copies, waits for them, and re-layouts: 155 us -> 189 us
    unnamed x515 -> x578, local copies, waits for them, and re-layouts: 16 us -> 50.3 us
  transfers between devices with their start and end apart: 3 -> 3, of which waited for: 2 -> 2; matrix products, arithmetic and copies ran while one was open for 13% -> 12% of each run, Pallas kernels for 0% -> 0%
where the time goes in v1:
time: 644 us; the launch traced here: 633 us
  waiting for transfers between devices  275 us (43%)
  local copies, waits for them, and re-layouts  189 us (29%)
  other arithmetic  114 us (18%)
  starting transfers between devices  23 us (4%)
  between operations  20.4 us (3%)
  matrix products  10.6 us (2%)
    psum x1, waiting for transfers between devices, per_device(): lax.psum(grid_whole, ('vol', 'dsg')).reshape(patches, control, control)  257 us
    unnamed x578, local copies, waits for them, and re-layouts  50.3 us
    mul x16, local copies, waits for them, and re-layouts, tensor_basis(): factor_x[:, None, None, :] * factor_y[None, :, None, :]  47 us
    sub x37, other arithmetic, precondition(): lax.linalg.tridiagonal_solve(below_diag, main_diag, above_diag, residual)  42 us
    concatenate x3, local copies, waits for them, and re-layouts, precondition(): lax.linalg.tridiagonal_solve(below_diag, main_diag, above_diag, residual)  35.3 us
    all_to_all x1, waiting for transfers between devices, per_device(): lax.all_to_all(picked, 'vol', split_axis=1, concat_axis=1, tiled=True)  18.1 us
  transfers between devices with their start and end apart: 3, of which 2 were waited for; matrix products, arithmetic and copies ran while one was open for 12% of the time, Pallas kernels for 0%

profile of v1, /device:TPU:2, one launch (start us, length us, event | category | flops | bytes accessed | tf_op | source)
XLA Modules:
  0.0 632.6 jit_solution(12258100428108970044)
XLA Ops:
  11.5 2.6 scatter_custom_fusion
  49.1 12.1 %all-to-all-start = ((s32[64,1,1,20]{3,2,1,0:T(1,128)}), s32[64,1,1,20]{3,2,1,0:T(1,128)S(1)}, u32[]{:S(2)}, u32[]{:S(2)}) async-start(s32[64,1,1,20]{3,2,1,0:T(1,128)} %constant_dynamic-update-slice_fusion), calls=%async_computation | async-start | bytes 65536 | tf_op jit(solution)/shard_map/all_to_all | solution.py:225
  103.2 4.6 mul.70848
  107.8 3.5 copy.10669
  111.3 4.4 mul.70860
  115.7 3.6 copy.10670
  119.3 4.4 mul.70872
  123.8 3.6 copy.10671
  127.3 3.8 mul.70882
  131.1 3.5 copy.10672
  135.0 7.6 %gather_fusion.2 = f32[2048,128]{1,0:T(8,128)} fusion(f32[4096,128]{1,0:T(8,128)S(1)} %copy-done, s32[2048]{0:T(1024)S(1)} %get-tuple-element.1886), kind=kCustom, calls=%fused_computation.2 | custom fusion | bytes 2105344 | tf_op jit(solution)/shard_map/while/body/eval_jaxpr/jit(_take)/gather | solution.py:197
  142.6 3.1 gather_fusion
  149.3 10.4 %all-to-all-start.1 = ((f32[128,64,20]{0,2,1:T(8,128)}), f32[128,64,20]{0,2,1:T(8,128)S(1)}, u32[]{:S(2)}, u32[]{:S(2)}) async-start(f32[128,64,20]{0,2,1:T(8,128)} %reshape.315128), calls=%async_computation.1 | async-start | bytes 1572864 | tf_op jit(solution)/shard_map/all_to_all | solution.py:230
  162.1 2.6 multiply_reduce_fusion.7
  165.0 18.1 %all-to-all-done.1 = f32[128,64,20]{0,2,1:T(8,128)S(1)} async-done(((f32[128,64,20]{0,2,1:T(8,128)}), f32[128,64,20]{0,2,1:T(8,128)S(1)}, u32[]{:S(2)}, u32[]{:S(2)}) %all-to-all-start.1) | async-done | bytes 655392 | tf_op jit(solution)/shard_map/all_to_all | solution.py:230
  183.0 3.8 multiply_reduce_fusion.8
  193.3 3.1 fusion.83
  197.2 257.4 %all-reduce.6.cloned.1.call-done = f32[96,64,64]{0,2,1:T(8,128)} async-done(((f32[96,64,64]{0,2,1:T(8,128)}), f32[96,64,64]{0,2,1:T(8,128)}) %all-reduce.6.cloned.1.call-update) | async-done | bytes 1572880 | tf_op jit(solution)/shard_map/psum | solution.py:248
  471.5 4.8 multiply_subtract_fusion.370
  476.4 9.9 %concatenate.199 = f32[63,96,64]{1,0,2:T(8,128)S(1)} concatenate(f32[1,96,64]{1,0,2:T(1,128)} %get-tuple-element.1229, f32[1,96,64]{1,0,2:T(1,128)} %get-tuple-element.1230, f32[1,96,64]{1,0,2:T(1,128)} %get-tuple-element.1231, f32[1,96,64]{1,0,2:T(1,128)} %get-tuple-element.1232, f32[1,96,64]{1,0,2:T(1,128)} %get-tuple-element.1233, f32[1,96,64]{1,0,2:T(1,128)} %get-tuple-element.1234, ...), dimensions={0} | concatenate | bytes 3096576 | tf_op jit(solution)/shard_map/vmap()/concatenate | solution.py:156
  497.8 3.3 fusion.11
  503.5 2.7 multiply_subtract_fusion.308
  510.6 2.7 broadcast_multiply_fusion.14
  529.0 3.0 fusion.7
  549.2 4.7 multiply_subtract_fusion.124
  553.9 15.6 %concatenate.207 = f32[63,96,64]{1,0,2:T(8,128)} concatenate(f32[1,96,64]{1,0,2:T(1,128)S(1)} %get-tuple-element.824, f32[1,96,64]{1,0,2:T(1,128)S(1)} %get-tuple-element.825, f32[1,96,64]{1,0,2:T(1,128)S(1)} %get-tuple-element.826, f32[1,96,64]{1,0,2:T(1,128)} %get-tuple-element.827, f32[1,96,64]{1,0,2:T(1,128)} %get-tuple-element.828, f32[1,96,64]{1,0,2:T(1,128)} %get-tuple-element.829, ...), dimensions={0} | concatenate | bytes 3096576 | tf_op jit(solution)/shard_map/vmap()/concatenate | solution.py:156
  580.5 3.0 fusion.3
  586.6 4.3 multiply_subtract_fusion.62
  603.5 4.9 multiply_subtract_fusion
  608.4 9.8 %concatenate.211 = f32[63,96,64]{1,0,2:T(8,128)S(1)} concatenate(f32[1,96,64]{1,0,2:T(1,128)S(1)} %get-tuple-element.660, f32[1,96,64]{1,0,2:T(1,128)S(1)} %get-tuple-element.661, f32[1,96,64]{1,0,2:T(1,128)S(1)} %get-tuple-element.662, f32[1,96,64]{1,0,2:T(1,128)} %get-tuple-element.663, f32[1,96,64]{1,0,2:T(1,128)} %get-tuple-element.664, f32[1,96,64]{1,0,2:T(1,128)} %get-tuple-element.665, ...), dimensions={0} | concatenate | bytes 3096576 | tf_op jit(solution)/shard_map/vmap()/concatenate | solution.py:156
  619.9 2.5 dynamic-slice_add_fusion
  622.3 3.2 copy.12215
  (958 shorter events, 185.4 us)
Async XLA Ops:
  7.2 127.8 %copy-start = (f32[4096,128]{1,0:T(8,128)S(1)}, f32[4096,128]{1,0:T(8,128)}, u32[]{:S(2)}) copy-start(f32[4096,128]{1,0:T(8,128)} %param.58) | copy-start | bytes 6291460
  11.5 64.3 %copy-start.118 = (s32[512,1]{0,1:T(1,128)}, s32[512,1]{0,1:T(1,128)S(1)}, u32[]{:S(2)}) copy-start(s32[512,1]{0,1:T(1,128)S(1)} %get-tuple-element.1371) | copy-start | bytes 6148
  49.1 85.7 %all-to-all-start = ((s32[64,1,1,20]{3,2,1,0:T(1,128)}), s32[64,1,1,20]{3,2,1,0:T(1,128)S(1)}, u32[]{:S(2)}, u32[]{:S(2)}) async-start(s32[64,1,1,20]{3,2,1,0:T(1,128)} %constant_dynamic-update-slice_fusion), calls=%async_computation | async-start | bytes 65536 | tf_op jit(solution)/shard_map/all_to_all | solution.py:225
  83.1 4.5 copy-start.119
  127.3 7.3 %copy-start.102 = (f32[3,512]{1,0:T(4,128)S(1)}, f32[3,512]{1,0:T(4,128)}, u32[]{:S(2)}) copy-start(f32[3,512]{1,0:T(4,128)} %get-tuple-element.1819) | copy-start | bytes 18436
  147.1 13.2 %copy-start.109 = (pred[2048]{0:T(1024)(128)(4,1)S(1)}, pred[2048]{0:T(1024)(128)(4,1)}, u32[]{:S(2)}) copy-start(pred[2048]{0:T(1024)(128)(4,1)} %compare_and_fusion) | copy-start | bytes 6148
  149.3 12.6 %copy-start.8 = (f32[64,2048]{0,1:T(8,128)S(1)}, f32[64,2048]{0,1:T(8,128)}, u32[]{:S(2)}) copy-start(f32[64,2048]{0,1:T(8,128)} %copy.10680) | copy-start | bytes 1572868
  149.3 33.7 %all-to-all-start.1 = ((f32[128,64,20]{0,2,1:T(8,128)}), f32[128,64,20]{0,2,1:T(8,128)S(1)}, u32[]{:S(2)}, u32[]{:S(2)}) async-start(f32[128,64,20]{0,2,1:T(8,128)} %reshape.315128), calls=%async_computation.1 | async-start | bytes 1572864 | tf_op jit(solution)/shard_map/all_to_all | solution.py:230
  159.8 294.8 %all-reduce.6.cloned.1.call-start = ((), (), s32[]{:S(2)}) async-start(), calls=%async_computation.2 | async-start | bytes 4194304 | tf_op jit(solution)/shard_map/psum | solution.py:248
  165.0 24.3 %copy-start.133 = (pred[512]{0:T(512)(128)(4,1)S(1)}, pred[512]{0:T(512)(128)(4,1)}, u32[]{:S(2)}) copy-start(pred[512]{0:T(512)(128)(4,1)} %get-tuple-element.1370) | copy-start | bytes 1540
  186.9 4.1 copy-start.79
  186.9 4.1 copy-start.123
  186.9 4.1 copy-start.124
  187.0 4.1 copy-start.125
  187.0 4.1 copy-start.126
  187.0 4.1 copy-start.127
  187.0 4.1 copy-start.128
  187.0 4.1 copy-start.129
  190.3 6.2 copy-start.122
  465.3 11.1 %copy-start.80 = (f32[96,64]{0,1:T(8,128)}, f32[96,64]{0,1:T(8,128)S(1)}, u32[]{:S(2)}) copy-start(f32[96,64]{0,1:T(8,128)S(1)} %get-tuple-element.1214) | copy-start | bytes 73732
  465.3 11.1 %copy-start.83 = (f32[96,64]{0,1:T(8,128)}, f32[96,64]{0,1:T(8,128)S(1)}, u32[]{:S(2)}) copy-start(f32[96,64]{0,1:T(8,128)S(1)} %get-tuple-element.1215) | copy-start | bytes 73732
  465.3 21.0 %copy-start.75 = (f32[96,64]{0,1:T(8,128)}, f32[96,64]{0,1:T(8,128)S(1)}, u32[]{:S(2)}) copy-start(f32[96,64]{0,1:T(8,128)S(1)} %get-tuple-element.1206) | copy-start | bytes 73732
  471.4 5.0 copy-start.11
  471.4 4.9 copy-start.15
  471.4 4.9 copy-start.19
  471.5 4.9 copy-start.23
  471.5 4.9 copy-start.27
  471.5 4.9 copy-start.31
  553.8 15.6 %copy-start.5 = (f32[96,64,64]{0,2,1:T(8,128)S(1)}, f32[96,64,64]{0,2,1:T(8,128)}, u32[]{:S(2)}) copy-start(f32[96,64,64]{0,2,1:T(8,128)} %copy-done.4) | copy-start | bytes 4718596
  553.8 15.6 %copy-start.86 = (f32[96,64]{0,1:T(8,128)S(1)}, f32[96,64]{0,1:T(8,128)}, u32[]{:S(2)}) copy-start(f32[96,64]{0,1:T(8,128)} %get-tuple-element.804) | copy-start | bytes 73732
  608.4 9.8 %copy-start.85 = (f32[96,64]{0,1:T(8,128)S(1)}, f32[96,64]{0,1:T(8,128)}, u32[]{:S(2)}) copy-start(f32[96,64]{0,1:T(8,128)} %get-tuple-element.640) | copy-start | bytes 73732
  619.9 5.6 copy-start.1
  (114 other events, 235.0 us)
Sparse Core Ops, SparseCore 0:
  196.6 257.9 all-reduce.5
